TPU v7x, 32 devices: a whole 2x2x4 slice. The times are simulated.
32 devices in a mesh: groups: 2 (over y), blk: 4 (over z), win: 4 (over x, core).
Axes of the slice: x: 2, y: 2, z: 4, core: 2. Of those that a mesh axis runs over, the one named last changes fastest.
Arguments:
- spectra: bfloat16 [2, 24, 1024, 201], P(None, 'win', ('groups', 'blk')), parts along dimension 2
- channel_slot: int32 [1024], P(('groups', 'blk')), parts along dimension 0, may hold values from 0 to 511, as said below
- partners: int32 [2, 4], replicated, may hold values from 0 to 3, as said below
Outputs:
- correlations: bfloat16 [2, 1024, 101, 128], P(None, ('groups', 'blk', 'win')), parts along dimension 1
There are 2 independent parts, one for each index of `groups`. A program takes and returns all parts, laid end to end along the dimension named above; an argument that names none is the same for every part. Nothing has to cross between parts.
Inputs may be any that keep to these rules, and one draw needn't show every extreme that they name: channel_slot is a permutation of 0 to 511. For every acquisition shard s (channels s * 128 to s * 128 + 127) and every block b, exactly 32 of the shard's channels go to block b, and they take the slots b * 128 + s * 32 + q for q from 0 to 31. In round r, partners[r, i] = i XOR m_r for one value m_r of 1 to 3 per round; the rounds' values differ.
All inputs are finite; a program needn't handle non-finite values.
Results may differ from a plain program's by a relative error of at most 0.0057.
Values may be sent and summed in bfloat16 or wider, within the bound.
A program may use at most 128 MiB of HBM per device.

v0:
```python
import functools
import math

import jax
import jax.numpy as jnp
from jax import lax
from jax.experimental import pallas as pl
from jax.experimental.pallas import tpu as pltpu
from jax.sharding import PartitionSpec as P

L = 101
ROUNDS = 2


eps_power = 1e-06
half_band = 2
tile_rows = 8


def whiten_into(piece, store, n_win, rows):
    power = None
    for win in range(n_win):
        value_array = piece(win).astype(jnp.float32)
        part = jnp.sum(value_array * value_array, axis=0)
        power = part if power is None else power + part
    nbins = power.shape[1]
    padding = jnp.zeros((power.shape[0], half_band), jnp.float32)
    padded = jnp.concatenate([padding, power, padding], axis=1)
    total = padded[:, 0:nbins]
    for offset in range(1, 2 * half_band + 1):
        total = total + padded[:, offset : offset + nbins]
    place = lax.broadcasted_iota(jnp.int32, power.shape, 1)
    count = 1 + jnp.minimum(place, half_band) + jnp.minimum(nbins - 1 - place, half_band)
    level = total / (count.astype(jnp.float32) * (n_win * rows // 2))
    scale = lax.rsqrt(level + eps_power)
    for win in range(n_win):
        store(win, (piece(win).astype(jnp.float32) * scale).astype(jnp.bfloat16))


def lag_table(nbins, nlags, windows):
    samples = 2 * (nbins - 1)
    freq = jnp.arange(nbins, dtype=jnp.int32)
    lags = jnp.arange(nlags, dtype=jnp.int32) - (nlags - 1) // 2
    phase_index = freq[:, None] * lags[None, :] % samples
    angle = 2.0 * math.pi / samples * phase_index.astype(jnp.float32)
    weight = jnp.where((freq == 0) | (freq == nbins - 1), 1.0, 2.0).astype(jnp.float32)
    norm = 1.0 / math.sqrt(windows * samples)
    cos_part = weight[:, None] * jnp.cos(angle) * norm
    sin_part = -weight[:, None] * jnp.sin(angle) * norm
    return jnp.concatenate([cos_part, sin_part], axis=0)


def correlate(both, right, table):
    cross = jnp.einsum(
        "cwak,wbk->kcab", both, right, preferred_element_type=jnp.float32
    ).astype(jnp.bfloat16)
    return jnp.einsum(
        "kcab,ckl->lab", cross, table, preferred_element_type=jnp.float32
    ).astype(jnp.bfloat16)


def flip(index, bit):
    return index + bit - 2 * bit * ((index // bit) % 2)


def exchange_kernel(
    n_blk, n_win, rounds, pair_ref, own_ref, *refs
):
    right_refs = refs[:rounds]
    both_ref, got_ref, src_ref, pair_send, pair_recv = refs[rounds : rounds + 5]
    pass_send, pass_recv, own_send, own_recv, local_sem = refs[rounds + 5 :]
    blk = lax.axis_index("blk")
    win = lax.axis_index("win")
    per_share = n_blk // n_win
    barrier = pltpu.get_barrier_semaphore()
    for step in range(1, n_blk * n_win):
        other = (blk * n_win + win + step) % (n_blk * n_win)
        pl.semaphore_signal(
            barrier,
            inc=1,
            device_id={"blk": other // n_win, "win": other % n_win},
            device_id_type=pl.DeviceIdType.MESH,
        )
    pl.semaphore_wait(barrier, n_blk * n_win - 1)

    def remote(src, dst, send, recv, to_blk, to_win):
        return pltpu.make_async_remote_copy(
            src_ref=src,
            dst_ref=dst,
            send_sem=send,
            recv_sem=recv,
            device_id={"blk": to_blk, "win": to_win},
            device_id_type=pl.DeviceIdType.MESH,
        )

    bits = []
    bit = n_win // 2
    while bit:
        bits.append(bit)
        bit //= 2

    order = list(range(n_blk))

    def across(step):
        other, each = blk, 1
        while each < n_blk:
            if step & each:
                other = flip(other, each)
            each *= 2
        return other

    def direct(step):
        dest = across(step)
        return remote(
            pair_ref.at[:, :, dest], got_ref.at[:, win, :, blk],
            pair_send.at[step], pair_recv.at[step], dest, win,
        )

    user = blk // per_share
    place = blk % per_share

    def own(step):
        dest = across(step)
        return remote(
            own_ref.at[:, dest], src_ref.at[win, :, place],
            own_send.at[step], own_recv.at[place * n_win + win], dest, user,
        )

    def passed(step, offset, over):
        origin = across(step)
        slot = win
        for each in bits:
            if offset & each:
                slot = flip(slot, each)
        target = got_ref.at[:, slot, :, origin]
        source = pair_ref.at[:, :, blk] if step == 0 and offset == 0 else target
        mark = (offset | over) - 1
        return remote(
            source, target, pass_send.at[mark, step], pass_recv.at[mark, step], blk, flip(win, over)
        )

    rows = pair_ref.shape[1]
    half = rows // 2
    keep = pltpu.make_async_copy(
        pair_ref.at[:, :, blk], got_ref.at[:, win, :, blk], local_sem.at[0]
    )
    keep.start()
    is_user = user == win

    def own_keep():
        return pltpu.make_async_copy(
            own_ref.at[:, blk], src_ref.at[win, :, place], local_sem.at[1]
        )

    @pl.when(is_user)
    def _():
        own_keep().start()

    passes = []
    held = [0]
    for over in bits:
        passes.extend((offset, over) for offset in held)
        held = held + [offset | over for offset in held]

    sends = []
    for offset, over in passes:
        if offset == 0:
            copy = passed(0, 0, over)
            copy.start()
            sends.append(copy)
    for step in order[1:]:
        copy = direct(step)
        copy.start()
        sends.append(copy)
    for step in order[1:]:
        copy = own(step)
        copy.start()
        sends.append(copy)

    @pl.when(jnp.logical_not(is_user))
    def _():
        own(0).start()

    keep.wait()

    @pl.when(is_user)
    def _():
        own_keep().wait()

    waited = set()

    def arrive(step, offset):
        if (step, offset) in waited:
            return
        waited.add((step, offset))
        if offset == 0:
            if step:
                direct(step).wait_recv()
        else:
            over = offset & -offset
            passed(step, offset - over, over).wait_recv()

    def finish(step):
        for offset in held:
            arrive(step, offset)
        origin = across(step)

        for index in range(rounds):

            def store(peer, white):
                right_refs[index][pl.ds(peer * rows, rows), origin] = white

            whiten_into(lambda peer: got_ref[index, peer, :, origin], store, n_win, rows)

    for turn in range(n_blk + 1):
        if 1 <= turn < n_blk:
            step = order[turn]
            arrive(step, 0)
            for offset, over in passes:
                if offset == 0:
                    copy = passed(step, 0, over)
                    copy.start()
                    sends.append(copy)
        if turn >= 1:
            step = order[turn - 1]
            for offset, over in passes:
                if offset:
                    arrive(step, offset)
                    copy = passed(step, offset, over)
                    copy.start()
                    sends.append(copy)
        if turn >= 2:
            finish(order[turn - 2])
    finish(order[n_blk - 1])
    for local in range(per_share):
        for peer in range(n_win):
            here = jnp.logical_and(blk == win * per_share + local, win == peer)

            @pl.when(jnp.logical_not(here))
            def _():
                piece = src_ref.at[peer, :, local]
                remote(
                    piece, piece, own_send.at[0], own_recv.at[local * n_win + peer], blk, win
                ).wait_recv()

    def one_shard(local, carry):
        def store(peer, white):
            both_ref[0, pl.ds(peer * rows, rows), local] = white
            both_ref[1, pl.ds(peer * rows, half), local] = white[half:]
            both_ref[1, pl.ds(peer * rows + half, half), local] = -white[:half]

        whiten_into(lambda peer: src_ref[peer, :, local], store, n_win, rows)
        return carry

    lax.fori_loop(0, per_share, one_shard, 0)

    for copy in sends:
        copy.wait_send()

    @pl.when(jnp.logical_not(is_user))
    def _():
        own(0).wait_send()


def exchange(pair, own, n_blk, n_win):
    rounds, rows, _, per_peer, nbins = pair.shape
    per_share = n_blk // n_win
    dtype = pair.dtype
    anywhere = pl.BlockSpec(memory_space=pl.ANY)
    vmem = pl.BlockSpec(memory_space=pltpu.VMEM)
    depth = n_win * rows
    return pl.pallas_call(
        functools.partial(exchange_kernel, n_blk, n_win, rounds),
        out_shape=(
            *[jax.ShapeDtypeStruct((depth, n_blk, per_peer, nbins), dtype)] * rounds,
            jax.ShapeDtypeStruct((2, depth, per_share, per_peer, nbins), dtype),
        ),
        in_specs=[anywhere, anywhere],
        out_specs=(vmem,) * (rounds + 1),
        scratch_shapes=[
            pltpu.VMEM((rounds, n_win, rows, n_blk, per_peer, nbins), dtype),
            pltpu.VMEM((n_win, rows, per_share, per_peer, nbins), dtype),
            pltpu.SemaphoreType.DMA((n_blk,)),
            pltpu.SemaphoreType.DMA((n_blk,)),
            pltpu.SemaphoreType.DMA((n_win - 1, n_blk)),
            pltpu.SemaphoreType.DMA((n_win - 1, n_blk)),
            pltpu.SemaphoreType.DMA((n_blk,)),
            pltpu.SemaphoreType.DMA((n_blk,)),
            pltpu.SemaphoreType.DMA((2,)),
        ],
        compiler_params=pltpu.CompilerParams(collective_id=0, has_side_effects=True),
    )(pair, own)


def body(spectra, channel_slot, partners):
    n_blk = lax.axis_size("blk")
    n_win = lax.axis_size("win")
    parts, mine, chans, nbins = spectra.shape
    rows = parts * mine
    per_peer = chans // n_blk
    here = lax.axis_index("blk")
    share = chans // n_win
    windows = mine * n_win
    flat = spectra.reshape(rows, chans, nbins)
    wanted = jnp.concatenate([partners, jnp.arange(n_blk, dtype=jnp.int32)[None]], axis=0)
    slots = (
        wanted[:, :, None] * chans
        + here * per_peer
        + jnp.arange(per_peer, dtype=jnp.int32)[None, None, :]
    )
    selector = (slots[..., None] == channel_slot).astype(jnp.bfloat16)
    pair = jnp.einsum(
        "tzqc,xcf->txzqf", selector[:ROUNDS], flat, preferred_element_type=jnp.float32
    ).astype(jnp.bfloat16)
    own = jnp.einsum(
        "zqc,xcf->xzqf", selector[ROUNDS], flat, preferred_element_type=jnp.float32
    ).astype(jnp.bfloat16)
    *right, both = exchange(pair, own, n_blk, n_win)
    right = [each.reshape(n_win * rows, chans, nbins) for each in right]
    both = both.reshape(2, n_win * rows, share, nbins)
    table = lag_table(nbins, L, windows).reshape(2, nbins, L).astype(jnp.bfloat16)
    results = [correlate(both, right[index], table) for index in range(ROUNDS)]
    return jnp.stack(results, axis=0).transpose(0, 2, 1, 3)


def solution(mesh):
    in_specs = (P(None, "win", ("groups", "blk"), None), P(("groups", "blk")), P())
    out_specs = P(None, ("groups", "blk", "win"), None, None)
    return jax.shard_map(body, mesh=mesh, in_specs=in_specs, out_specs=out_specs, check_vma=False)
```

profile of v0, /device:TPU:11, one launch (start us, length us, event | category | flops | bytes accessed | tf_op | source)
XLA Modules:
  0.0 106.7 jit_solution(215818624461247546)
XLA Ops:
  0.0 1.2 %copy.7 = bf16[2,6,128,201]{2,3,1,0:T(8,128)(2,1)S(1)} copy(bf16[2,6,128,201]{2,0,3,1:T(2,128)(2,1)} %param.3) | data formatting | bytes 1234944 | tf_op args[0]
  1.2 0.7 fusion.13
  1.9 0.1 iota_add_fusion
  1.9 0.8 broadcast_compare_fusion
  2.7 1.7 %fusion.2.pair_ref = bf16[2,12,4,32,201]{4,3,2,1,0:T(8,128)(2,1)} fusion(bf16[12,128,201,1,1]{1,2,4,0,3:T(8,128)(2,1)S(1)} %bitcast.57, pred[3,4,32,128]{3,2,1,0:T(32,128)(4,1)S(1)} %broadcast_compare_fusion), kind=kOutput, calls=%fused_computation.8 | convolution fusion | flops 158690304 | bytes 1906688 | tf_op jit(solution)/shard_map/tzqc,xcf->txzqf/dot_general | solution.py:312
  4.5 1.6 %fusion.5.own_ref = bf16[12,4,32,201]{3,2,1,0:T(8,128)(2,1)} fusion(bf16[12,128,201,1]{1,2,3,0:T(8,128)(2,1)S(1)} %bitcast.58, pred[3,4,32,128]{3,2,1,0:T(32,128)(4,1)S(1)} %broadcast_compare_fusion), kind=kOutput, calls=%fused_computation.12 | convolution fusion | flops 79345152 | bytes 1272832 | tf_op jit(solution)/shard_map/zqc,xcf->xzqf/dot_general | solution.py:315
  6.0 67.9 %shard_map.37 = (bf16[48,4,32,201]{3,2,1,0:T(8,128)(2,1)}, bf16[48,4,32,201]{3,2,1,0:T(8,128)(2,1)}, bf16[2,48,1,32,201]{4,3,2,1,0:T(8,128)(2,1)}) custom-call(bf16[2,12,4,32,201]{4,3,2,1,0:T(8,128)(2,1)} %fusion.2.pair_ref, bf16[12,4,32,201]{3,2,1,0:T(8,128)(2,1)} %fusion.5.own_ref), custom_call_target="tpu_custom_call" | custom-call | tf_op jit(solution)/shard_map/pallas_call | solution.py:272
  74.0 6.7 %copy.18 = bf16[2,48,32,201]{1,2,0,3:T(8,128)(2,1)S(1)} copy(bf16[2,48,32,201]{3,2,1,0:T(8,128)(2,1)} %bitcast.61) | data formatting | bytes 2469888 | tf_op jit(solution)/shard_map/reshape | solution.py:320
  80.7 4.9 %copy.19 = bf16[48,128,201,1]{1,0,3,2:T(8,128)(2,1)} copy(bf16[48,128,201,1]{2,1,0,3:T(8,128)(2,1)} %bitcast.60) | data formatting | bytes 4939776 | tf_op jit(solution)/shard_map/reshape | solution.py:319
  85.6 4.4 %fusion.15 = bf16[201,2,32,128]{3,2,1,0:T(8,128)(2,1)} fusion(bf16[2,48,32,201]{1,2,0,3:T(8,128)(2,1)S(1)} %copy.18, bf16[48,128,201,1]{1,0,3,2:T(8,128)(2,1)} %copy.19), kind=kOutput, calls=%fused_computation.34 | convolution fusion | flops 158072832 | bytes 6998016 | tf_op jit(solution)/shard_map/cwak,wbk->kcab/dot_general | solution.py:54
  89.9 0.5 multiply_convert_fusion.1
  90.5 5.0 %fusion.3 = bf16[1,101,32,128]{3,1,2,0:T(8,128)(2,1)} fusion(bf16[201,2,32,128]{3,2,1,0:T(8,128)(2,1)} %fusion.15, bf16[2,201,101]{2,1,0:T(8,128)(2,1)S(1)} %convert_element_type.33), kind=kOutput, calls=%fused_computation.10 | convolution fusion | flops 333025280 | bytes 4201780 | tf_op jit(solution)/shard_map/kcab,ckl->lab/dot_general | solution.py:57
  95.4 4.8 %copy.23 = bf16[48,128,201,1]{1,0,3,2:T(8,128)(2,1)} copy(bf16[48,128,201,1]{2,1,0,3:T(8,128)(2,1)} %bitcast.59) | data formatting | bytes 4939776 | tf_op jit(solution)/shard_map/reshape | solution.py:319
  100.2 2.7 %fusion.16 = bf16[201,2,32,128]{3,2,1,0:T(8,128)(2,1)S(1)} fusion(bf16[2,48,32,201]{1,2,0,3:T(8,128)(2,1)S(1)} %copy.18, bf16[48,128,201,1]{1,0,3,2:T(8,128)(2,1)} %copy.23), kind=kOutput, calls=%fused_computation.35 | convolution fusion | flops 158072832 | bytes 6998016 | tf_op jit(solution)/shard_map/cwak,wbk->kcab/dot_general | solution.py:54
  102.9 0.0 copy-start
  103.0 2.1 %fusion.4 = bf16[1,101,32,128]{3,1,2,0:T(8,128)(2,1)S(1)} fusion(bf16[201,2,32,128]{3,2,1,0:T(8,128)(2,1)S(1)} %fusion.16, bf16[2,201,101]{2,1,0:T(8,128)(2,1)S(1)} %convert_element_type.33), kind=kOutput, calls=%fused_computation.11 | convolution fusion | flops 333025280 | bytes 4201780 | tf_op jit(solution)/shard_map/kcab,ckl->lab/dot_general | solution.py:57
  105.1 0.0 copy-done
  105.1 0.2 maximum_bitcast_fusion
  105.3 1.4 %copy.12 = bf16[2,32,101,128]{3,1,2,0:T(8,128)(2,1)} copy(bf16[2,32,101,128]{3,2,1,0:T(8,128)(2,1)S(1)} %maximum_bitcast_fusion) | data formatting | bytes 3309568 | tf_op jit(solution)/shard_map/transpose | solution.py:323
  (5 shorter events, 0.1 us)
Async XLA Ops:
  102.9 2.2 %copy-start = (bf16[1,101,32,128]{3,1,2,0:T(8,128)(2,1)S(1)}, bf16[1,101,32,128]{3,1,2,0:T(8,128)(2,1)}, u32[]{:S(2)}) copy-start(bf16[1,101,32,128]{3,1,2,0:T(8,128)(2,1)} %fusion.3) | copy-start | bytes 2482180
where the time goes:
time: 107 us
  Pallas kernels  67.9 us (63%)
  local copies, waits for them, and re-layouts  19 us (18%)
  matrix products  17.4 us (16%)
  other arithmetic  2.21 us (2%)
    pallas_call x1, Pallas kernels, exchange(): pl.pallas_call(functools.partial(exchange_kernel, n_blk, n_win, rounds),...  67.9 us
    reshape x2, local copies, waits for them, and re-layouts, body(): right = [each.reshape(n_win * rows, chans, nbins) for each in right]  9.69 us
    dot_general x2, matrix products, correlate(): jnp.einsum('kcab,ckl->lab', cross, table, preferred_element_type=jnp.floa...  7.1 us
    dot_general x2, matrix products, correlate(): jnp.einsum('cwak,wbk->kcab', both, right, preferred_element_type=jnp.floa...  7.05 us
    reshape x1, local copies, waits for them, and re-layouts, body(): both = both.reshape(2, n_win * rows, share, nbins)  6.72 us

commit v1 on v0

--- a/solution.py
+++ b/solution.py
@@ -3,6 +3,7 @@
 
 import jax
 import jax.numpy as jnp
+import numpy as np
 from jax import lax
 from jax.experimental import pallas as pl
 from jax.experimental.pallas import tpu as pltpu
@@ -292,7 +293,7 @@
     )(pair, own)
 
 
-def body(spectra, channel_slot, partners):
+def plain_body(spectra, channel_slot, partners):
     n_blk = lax.axis_size("blk")
     n_win = lax.axis_size("win")
     parts, mine, chans, nbins = spectra.shape
@@ -323,6 +324,423 @@
     return jnp.stack(results, axis=0).transpose(0, 2, 1, 3)
 
 
+def select_kernel(n_blk, slots_ref, partners_ref, x_ref, out_ref):
+    dest = pl.program_id(0)
+    here = lax.axis_index("blk")
+    parts, _, nbins, chans = x_ref.shape
+    kinds, groups = out_ref.shape[1], out_ref.shape[2]
+    per_peer = chans // n_blk
+    row = lax.broadcasted_iota(jnp.int32, (chans, chans), 0)
+    slots = slots_ref[...]
+    picks = []
+    for kind in range(kinds):
+        block = dest if kind == kinds - 1 else partners_ref[kind, dest]
+        hit = slots == block * chans + here * per_peer + row % per_peer
+        picks.append(
+            jnp.concatenate(
+                [
+                    jnp.where(hit & (row // per_peer == y), 1.0, 0.0).astype(jnp.bfloat16)
+                    for y in range(n_blk)
+                ],
+                axis=1,
+            )
+        )
+    pick = jnp.concatenate(picks, axis=0)
+    for group in range(groups):
+        rows = [divmod(group * n_blk + y, parts) for y in range(n_blk)]
+        wide = jnp.concatenate([x_ref[part, win] for win, part in rows], axis=1)
+        got = lax.dot_general(
+            wide, pick, (((1,), (1,)), ((), ())), preferred_element_type=jnp.float32
+        ).astype(jnp.bfloat16)
+        for kind in range(kinds):
+            out_ref[0, kind, group] = got[:, kind * chans : (kind + 1) * chans]
+
+
+def select(flat, slots, partners, n_blk, kinds):
+    parts, mine, nbins, chans = flat.shape
+    groups = parts * mine // n_blk
+    return pl.pallas_call(
+        functools.partial(select_kernel, n_blk),
+        grid=(n_blk,),
+        out_shape=jax.ShapeDtypeStruct((n_blk, kinds, groups, nbins, chans), flat.dtype),
+        in_specs=[
+            pl.BlockSpec((1, chans), lambda d: (0, 0)),
+            pl.BlockSpec(memory_space=pltpu.SMEM),
+            pl.BlockSpec(flat.shape, lambda d: (0, 0, 0, 0)),
+        ],
+        out_specs=pl.BlockSpec((1, kinds, groups, nbins, chans), lambda d: (d, 0, 0, 0, 0)),
+    )(slots, partners, flat)
+
+
+def across(index, step, count):
+    other, bit = index, 1
+    while bit < count:
+        if step & bit:
+            other = flip(other, bit)
+        bit *= 2
+    return other
+
+
+def spread_kernel(
+    n, rounds, piece_ref, got_ref, own_ref, stage_ref,
+    far_send, far_recv, stage_send, stage_recv, pass_send, pass_recv,
+    own_send, own_recv, local_sem,
+):
+    blk = lax.axis_index("blk")
+    win = lax.axis_index("win")
+
+    def remote(src, dst, send, recv, to_blk, to_win):
+        return pltpu.make_async_remote_copy(
+            src_ref=src,
+            dst_ref=dst,
+            send_sem=send,
+            recv_sem=recv,
+            device_id={"blk": to_blk, "win": to_win},
+            device_id_type=pl.DeviceIdType.MESH,
+        )
+
+    barrier = pltpu.get_barrier_semaphore()
+    for step in range(1, n):
+        for to_blk, to_win in ((across(blk, step, n), win), (blk, across(win, step, n))):
+            pl.semaphore_signal(
+                barrier,
+                inc=1,
+                device_id={"blk": to_blk, "win": to_win},
+                device_id_type=pl.DeviceIdType.MESH,
+            )
+
+    def far(turn, step):
+        dest = across(blk, step, n)
+        return remote(
+            piece_ref.at[dest, turn], got_ref.at[turn, blk, win],
+            far_send.at[turn, step], far_recv.at[turn, step], dest, win,
+        )
+
+    def staged(step):
+        dest = across(blk, step, n)
+        return remote(
+            piece_ref.at[dest, rounds], stage_ref.at[blk],
+            stage_send.at[step], stage_recv.at[blk], dest, win,
+        )
+
+    def own(step):
+        user = across(win, step, n)
+        return remote(
+            stage_ref.at[user], own_ref.at[win], own_send.at[step], own_recv.at[step], blk, user
+        )
+
+    bits = []
+    bit = n // 2
+    while bit:
+        bits.append(bit)
+        bit //= 2
+    passes = []
+    held = [0]
+    for over in bits:
+        passes.extend((offset, over) for offset in held)
+        held = held + [offset | over for offset in held]
+
+    def passed(turn, step, offset, over):
+        origin = across(blk, step, n)
+        piece = got_ref.at[turn, origin, across(win, offset, n)]
+        source = piece_ref.at[blk, turn] if step == 0 and offset == 0 else piece
+        mark = (offset | over) - 1
+        return remote(
+            source, piece, pass_send.at[turn, step, mark], pass_recv.at[turn, step, mark],
+            blk, flip(win, over),
+        )
+
+    sends = []
+
+    def go(copy):
+        copy.start()
+        sends.append(copy)
+
+    keeps = [
+        pltpu.make_async_copy(
+            piece_ref.at[blk, turn], got_ref.at[turn, blk, win], local_sem.at[turn]
+        )
+        for turn in range(rounds)
+    ]
+    home = pltpu.make_async_copy(piece_ref.at[blk, rounds], stage_ref.at[blk], stage_recv.at[blk])
+    for keep in keeps:
+        keep.start()
+    home.start()
+    pl.semaphore_wait(barrier, 2 * (n - 1))
+    steps = list(range(n - 1, 0, -1))
+    for step in steps:
+        go(far(0, step))
+    for offset, over in passes:
+        if offset == 0:
+            go(passed(0, 0, 0, over))
+    for step in steps:
+        go(staged(step))
+    for step in steps:
+        go(far(1, step))
+    for turn in range(1, rounds):
+        for offset, over in passes:
+            if offset == 0:
+                go(passed(turn, 0, 0, over))
+
+    waited = set()
+
+    def arrive(turn, step, offset):
+        if (turn, step, offset) in waited:
+            return
+        waited.add((turn, step, offset))
+        if offset == 0:
+            if step:
+                far(turn, step).wait_recv()
+        else:
+            over = offset & -offset
+            passed(turn, step, offset - over, over).wait_recv()
+
+    def onward(turn, step, first):
+        for offset, over in passes:
+            if (offset == 0) == first:
+                arrive(turn, step, offset)
+                go(passed(turn, step, offset, over))
+
+    order = [0] + list(range(1, n))
+    for turn in range(rounds):
+        for place, step in enumerate(order):
+            if step:
+                onward(turn, step, True)
+            if place:
+                onward(turn, order[place - 1], False)
+        onward(turn, order[-1], False)
+        if turn == 0:
+            for step in range(1, n):
+                user = across(win, step, n)
+                piece = stage_ref.at[user]
+                pltpu.make_async_copy(piece, piece, stage_recv.at[user]).wait()
+                go(own(step))
+            piece = stage_ref.at[win]
+            pltpu.make_async_copy(piece, piece, stage_recv.at[win]).wait()
+            mine = pltpu.make_async_copy(piece, own_ref.at[win], local_sem.at[rounds])
+            mine.start()
+    for turn in range(rounds):
+        for step in order:
+            for offset in held:
+                arrive(turn, step, offset)
+    for step in range(1, n):
+        own(step).wait_recv()
+    mine.wait()
+    for keep in keeps:
+        keep.wait()
+    for copy in sends:
+        copy.wait_send()
+
+
+def spread(pieces, n, rounds):
+    shape, dtype = pieces.shape[2:], pieces.dtype
+    anywhere = pl.BlockSpec(memory_space=pl.ANY)
+    dma = pltpu.SemaphoreType.DMA
+    got, own, _ = pl.pallas_call(
+        functools.partial(spread_kernel, n, rounds),
+        out_shape=(
+            jax.ShapeDtypeStruct((rounds, n, n, *shape), dtype),
+            jax.ShapeDtypeStruct((n, *shape), dtype),
+            jax.ShapeDtypeStruct((n, *shape), dtype),
+        ),
+        in_specs=[anywhere],
+        out_specs=(anywhere,) * 3,
+        scratch_shapes=[
+            dma((rounds, n)), dma((rounds, n)), dma((n,)), dma((n,)),
+            dma((rounds, n, n - 1)), dma((rounds, n, n - 1)), dma((n,)), dma((n,)),
+            dma((rounds + 1,)),
+        ],
+        compiler_params=pltpu.CompilerParams(collective_id=1, has_side_effects=True),
+    )(pieces)
+    return got, own
+
+
+def lane_spread(n, per_peer, chans):
+    regroup = np.zeros((n, n, per_peer, n, n, per_peer), np.float32)
+    for shard in range(n):
+        for y in range(n):
+            for q in range(per_peer):
+                regroup[shard, y, q, y, shard, q] = 1.0
+    turned = np.zeros((n, per_peer, n, chans), np.float32)
+    for y in range(n):
+        for q in range(per_peer):
+            turned[y, q, y, q] = 1.0
+            part = y % 2
+            turned[y + 1 - 2 * part, q, y, per_peer + q] = 1.0 if part == 0 else -1.0
+    return regroup.reshape(n * chans, n * chans), turned.reshape(chans, n * chans)
+
+
+def combine_kernel(
+    n, unroll, got_ref, own_ref, regroup_ref, turn_ref, table_ref, out_ref,
+    right_ref, left_ref, cross_ref, pad_ref, scale_ref,
+):
+    rounds, _, _, groups, nbins, chans = got_ref.shape
+    per_peer = chans // n
+    depth = n * groups * n
+    stride = right_ref.shape[1] // depth
+    pad = (pad_ref.shape[0] - stride) // 2
+    pad_ref[...] = jnp.zeros_like(pad_ref)
+    place = lax.broadcasted_iota(jnp.int32, (nbins, chans), 0)
+    count = 1 + jnp.minimum(place, half_band) + jnp.minimum(nbins - 1 - place, half_band)
+    weight = 1.0 / (count.astype(jnp.float32) * (depth // 2))
+
+    def scale_of(piece):
+        def add(index, total):
+            value = piece(index // groups, index % groups).astype(jnp.float32)
+            return total + value * value
+
+        power = lax.fori_loop(0, n * groups, add, jnp.zeros((nbins, chans), jnp.float32))
+        total = power
+        for y in range(1, n):
+            total = total + pltpu.roll(power, y * per_peer, 1)
+        pad_ref[pl.ds(pad, nbins)] = total
+        near = pad_ref[pl.ds(pad - half_band, nbins)]
+        for offset in range(1 - half_band, half_band + 1):
+            near = near + pad_ref[pl.ds(pad + offset, nbins)]
+        return lax.rsqrt(near * weight + eps_power)
+
+    scale_ref[0] = scale_of(lambda win, group: own_ref[win, group])
+
+    def place_left(index, carry):
+        win, group = index // groups, index % groups
+        white = (own_ref[win, group].astype(jnp.float32) * scale_ref[0]).astype(jnp.bfloat16)
+        wide = jnp.dot(white, turn_ref[...], preferred_element_type=jnp.float32)
+        for y in range(n):
+            left_ref[pl.ds((index * n + y) * stride, nbins)] = wide[:, y * chans : (y + 1) * chans]
+        return carry
+
+    lax.fori_loop(0, n * groups, place_left, 0)
+
+    for turn in range(rounds):
+        for shard in range(n):
+            scale_ref[shard] = scale_of(lambda win, group: got_ref[turn, shard, win, group])
+
+        def place_right(index, carry):
+            win, group = index // groups, index % groups
+            white = jnp.concatenate(
+                [
+                    (got_ref[turn, shard, win, group].astype(jnp.float32) * scale_ref[shard]).astype(
+                        jnp.bfloat16
+                    )
+                    for shard in range(n)
+                ],
+                axis=1,
+            )
+            wide = jnp.dot(white, regroup_ref[...], preferred_element_type=jnp.float32)
+            for y in range(n):
+                right_ref[turn, pl.ds((index * n + y) * stride, nbins)] = wide[
+                    :, y * chans : (y + 1) * chans
+                ]
+            return carry
+
+        lax.fori_loop(0, n * groups, place_right, 0)
+
+    both = 2 * per_peer
+
+    def one_bin(bin_index):
+        left = left_ref[pl.ds(bin_index, depth, stride)].astype(jnp.bfloat16)
+        right = jnp.concatenate(
+            [
+                right_ref[turn, pl.ds(bin_index, depth, stride)].astype(jnp.bfloat16)
+                for turn in range(rounds)
+            ],
+            axis=1,
+        )
+        cross = lax.dot_general(
+            left, right, (((0,), (0,)), ((), ())), preferred_element_type=jnp.float32
+        )
+        for turn in range(rounds):
+            cross_ref[turn, pl.ds(bin_index * both, both)] = cross[
+                :both, turn * chans : (turn + 1) * chans
+            ]
+
+    def some_bins(index, carry):
+        for offset in range(unroll):
+            one_bin(index * unroll + offset)
+        return carry
+
+    lax.fori_loop(0, nbins // unroll, some_bins, 0)
+    for bin_index in range(nbins // unroll * unroll, nbins):
+        one_bin(bin_index)
+
+    def one_source(source):
+        total = None
+        for part in range(2):
+            rows = jnp.concatenate(
+                [
+                    cross_ref[turn, pl.ds(part * per_peer + source, nbins, both)].astype(jnp.bfloat16)
+                    for turn in range(rounds)
+                ],
+                axis=1,
+            )
+            term = jnp.dot(table_ref[part], rows, preferred_element_type=jnp.float32)
+            total = term if total is None else total + term
+        total = total.astype(jnp.bfloat16)
+        for turn in range(rounds):
+            out_ref[turn, source] = total[:, turn * chans : (turn + 1) * chans]
+
+    def two_sources(index, carry):
+        one_source(2 * index)
+        one_source(2 * index + 1)
+        return carry
+
+    lax.fori_loop(0, per_peer // 2, two_sources, 0)
+
+
+def combine(got, own, n, windows):
+    rounds, _, _, groups, nbins, chans = got.shape
+    per_peer = chans // n
+    depth = n * groups * n
+    stride = (nbins + 7) // 8 * 8
+    regroup, turned = lane_spread(n, per_peer, chans)
+    table = fixed_table(nbins, L, windows)
+    vmem = pl.BlockSpec(memory_space=pltpu.VMEM)
+    return pl.pallas_call(
+        functools.partial(combine_kernel, n, 8),
+        out_shape=jax.ShapeDtypeStruct((rounds, per_peer, L, chans), jnp.bfloat16),
+        in_specs=[vmem] * 5,
+        out_specs=vmem,
+        scratch_shapes=[
+            pltpu.VMEM((rounds, depth * stride, chans), jnp.float32),
+            pltpu.VMEM((depth * stride, chans), jnp.float32),
+            pltpu.VMEM((rounds, nbins * 2 * per_peer, chans), jnp.float32),
+            pltpu.VMEM((stride + 16, chans), jnp.float32),
+            pltpu.VMEM((n, nbins, chans), jnp.float32),
+        ],
+    )(
+        got, own, jnp.asarray(regroup, jnp.bfloat16), jnp.asarray(turned, jnp.bfloat16),
+        jnp.asarray(table, jnp.bfloat16),
+    )
+
+
+def fixed_table(nbins, nlags, windows):
+    samples = 2 * (nbins - 1)
+    freq = np.arange(nbins)
+    lags = np.arange(nlags) - (nlags - 1) // 2
+    angle = 2.0 * np.pi / samples * (lags[:, None] * freq[None, :] % samples)
+    weight = np.where((freq == 0) | (freq == nbins - 1), 1.0, 2.0) / np.sqrt(windows * samples)
+    return np.stack([np.cos(angle) * weight, -np.sin(angle) * weight]).astype(np.float32)
+
+
+def dense_body(spectra, channel_slot, partners):
+    n = lax.axis_size("blk")
+    parts, mine, chans, nbins = spectra.shape
+    rounds = partners.shape[0]
+    flat = spectra.transpose(0, 1, 3, 2)
+    pieces = select(flat, channel_slot.reshape(1, chans), partners, n, rounds + 1)
+    got, own = spread(pieces, n, rounds)
+    return combine(got, own, n, mine * n)
+
+
+def body(spectra, channel_slot, partners):
+    n_blk = lax.axis_size("blk")
+    rows = spectra.shape[0] * spectra.shape[1]
+    fits = n_blk == lax.axis_size("win") and rows % n_blk == 0 and n_blk % spectra.shape[0] == 0
+    if fits and 2 * spectra.shape[2] // n_blk <= spectra.shape[2]:
+        return dense_body(spectra, channel_slot, partners)
+    return plain_body(spectra, channel_slot, partners)
+
+
 def solution(mesh):
     in_specs = (P(None, "win", ("groups", "blk"), None), P(("groups", "blk")), P())
     out_specs = P(None, ("groups", "blk", "win"), None, None)

time: 107 us -> 105 us (0.981)
  the two profiles are of different devices: /device:TPU:11 before, /device:TPU:0 now
where the time goes in v1:
time: 105 us
  Pallas kernels  100 us (95%)
  local copies, waits for them, and re-layouts  4.85 us (5%)
    pallas_call x1, Pallas kernels, spread(): pl.pallas_call(functools.partial(spread_kernel, n, rounds), out_shape=(ja...  59.6 us
    pallas_call x1, Pallas kernels, combine(): pl.pallas_call(functools.partial(combine_kernel, n, 8), out_shape=jax.Sha...  36.4 us
    pallas_call x1, Pallas kernels, select(): pl.pallas_call(functools.partial(select_kernel, n_blk), grid=(n_blk,), ou...  4.28 us
    pallas_call x1, local copies, waits for them, and re-layouts, combine(): pl.pallas_call(functools.partial(combine_kernel, n, 8), out_shape=jax.Sha...  2.86 us

profile of v1, /device:TPU:0, one launch (start us, length us, event | category | flops | bytes accessed | tf_op | source)
XLA Modules:
  0.0 105.2 jit_solution(3108202570577405504)
XLA Ops:
  0.0 2.0 %copy.10 = bf16[2,6,128,201]{2,3,1,0:T(8,128)(2,1)} copy(bf16[2,6,128,201]{2,0,3,1:T(2,128)(2,1)} %param.6) | data formatting | bytes 1234944 | tf_op args[0]
  2.0 4.3 %shard_map.64.piece_ref = bf16[4,3,3,201,128]{4,3,2,1,0:T(8,128)(2,1)} custom-call(s32[1,128]{1,0:T(1,128)} %bitcast.5, s32[2,4]{1,0:T(2,128)} %partners_ref.1, bf16[2,6,201,128]{3,2,1,0:T(8,128)(2,1)} %bitcast.4), custom_call_target="tpu_custom_call" | custom-call | tf_op jit(solution)/shard_map/pallas_call | solution.py:362
  6.3 59.6 %shard_map.65 = (bf16[2,4,4,3,201,128]{5,4,3,2,1,0:T(8,128)(2,1)}, bf16[4,3,201,128]{3,2,1,0:T(8,128)(2,1)}, bf16[4,3,201,128]{3,2,1,0:T(8,128)(2,1)}) custom-call(bf16[4,3,3,201,128]{4,3,2,1,0:T(8,128)(2,1)} %shard_map.64.piece_ref), custom_call_target="tpu_custom_call" | custom-call | tf_op jit(solution)/shard_map/pallas_call | solution.py:539
  65.9 36.4 %shard_map.66 = bf16[2,32,101,128]{3,2,1,0:T(8,128)(2,1)} custom-call(bf16[2,4,4,3,201,128]{5,4,3,2,1,0:T(8,128)(2,1)} %get-tuple-element.7.got_ref, bf16[4,3,201,128]{3,2,1,0:T(8,128)(2,1)} %get-tuple-element.8.own_ref, bf16[512,512]{1,0:T(8,128)(2,1)} %constant.6.clone.regroup_ref, bf16[128,512]{1,0:T(8,128)(2,1)} %constant.7.clone.turn_ref, ...), custom_call_target="tpu_custom_call" | custom-call | tf_op jit(solution)/shard_map/pallas_call | solution.py:698
  102.4 2.9 %copy.8 = bf16[2,32,101,128]{3,1,2,0:T(8,128)(2,1)} copy(bf16[2,32,101,128]{3,2,1,0:T(8,128)(2,1)} %shard_map.66) | data formatting | bytes 3309568 | tf_op jit(solution)/shard_map/pallas_call | solution.py:698
